TPU v7x, 128 devices: a whole 4x4x4 slice. The times are simulated.
128 devices in a mesh: dom: 32 (over x_lo, z, y), rep: 4 (over x_hi, core).
Axes of the slice: x: 4 (x_hi: 2, x_lo: 2; x = x_hi * 2 + x_lo), y: 4, z: 4, core: 2. Of those that a mesh axis runs over, the one named last changes fastest.
Arguments:
- features: bfloat16 [49152, 256], P('dom'), may hold values from -6 to 6
- tile_weights: bfloat16 [32, 4, 8, 88, 128, 128], P('dom', 'rep'), may hold values from 0 to 0.0115356445
- tile_rows: int32 [32, 4, 8, 88], P('dom', 'rep'), may hold values from 0 to 11, as said below
- tile_cols: int32 [32, 4, 8, 88], P('dom', 'rep'), may hold values from 0 to 11, as said below
- tile_counts: int32 [32, 4, 8], P('dom', 'rep'), may hold values from 1 to 88, as said below
- weight_self: bfloat16 [256, 256], replicated, may hold values from -0.375 to 0.375
- weight_neigh: bfloat16 [256, 256], replicated, may hold values from -0.375 to 0.375
- cotangent: bfloat16 [49152, 256], P(('dom', 'rep')), may hold values from -0.026977539 to 0.026977539
Outputs:
- out: bfloat16 [49152, 256], P(('dom', 'rep'))
- grad_self: float32 [256, 256], replicated
- grad_neigh: float32 [256, 256], replicated
Inputs may be any that keep to these rules, and one draw needn't show every extreme that they name: For each p, r, s the first tile_counts[p, r, s] slots name distinct pairs (tile_rows, tile_cols); slots from tile_counts[p, r, s] on are unused. `tile_cols`: see tile_rows. `tile_counts`: some device fills all 88 slots of some column step.
All inputs are finite; a program needn't handle non-finite values.
Results may differ from a plain program's by a relative error of at most 0.0052.
Values may be sent and summed in bfloat16 or wider, within the bound.
A program may use at most 128 MiB of HBM per device.

v0:
```python
import jax
import jax.numpy as jnp
from jax import lax
from jax.sharding import PartitionSpec as P


def passed_along(block, axis, distance):
    devices = range(lax.axis_size(axis))
    route = [((i - distance) % len(devices), i) for i in devices]
    return lax.ppermute(block, axis, route)


def step_terms(feature_block, weights_dev, rows_dev, cols_dev, counts_dev, column_step):
    weights_now = lax.dynamic_index_in_dim(weights_dev, column_step, 0, keepdims=False)
    row_index = lax.dynamic_index_in_dim(rows_dev, column_step, 0, keepdims=False)
    col_index = lax.dynamic_index_in_dim(cols_dev, column_step, 0, keepdims=False)
    live_total = lax.dynamic_index_in_dim(counts_dev, column_step, 0, keepdims=False)
    slot_total = weights_now.shape[0]
    tile_side = weights_now.shape[1]
    width = feature_block.shape[1]
    row_tiles = feature_block.shape[0] // tile_side
    flat_block = feature_block.reshape(row_tiles, tile_side * width)
    tile_ids = jnp.arange(row_tiles, dtype=jnp.int32)
    select = (col_index[:, None] == tile_ids[None, :]).astype(jnp.bfloat16)
    picked = jnp.dot(select, flat_block, preferred_element_type=jnp.float32).astype(jnp.bfloat16)
    picked = picked.reshape(slot_total, tile_side, width)
    product = jnp.einsum("kij,kjf->kif", weights_now, picked, preferred_element_type=jnp.float32)
    live_slots = jnp.arange(slot_total, dtype=jnp.int32) < live_total
    placing = ((row_index[None, :] == tile_ids[:, None]) & live_slots[None, :]).astype(jnp.float32)
    summed = jnp.dot(
        placing,
        product.reshape(slot_total, tile_side * width),
        precision=lax.Precision.HIGHEST,
        preferred_element_type=jnp.float32,
    )
    return summed.reshape(feature_block.shape[0], width)


def rotate(feature_block, steps_per_group, offset, direction_sign):
    replica = lax.axis_index("rep")
    bit_total = (lax.axis_size("rep") - 1).bit_length()
    domain = lax.axis_size("dom")
    moves = []
    moves.append((offset % domain, -1))
    for bit_number in range(bit_total):
        moves.append((direction_sign * steps_per_group * (1 << bit_number) % domain, bit_number))
    for amount, bit_number in moves:
        shifted = passed_along(feature_block, "dom", amount)
        if bit_number < 0:
            feature_block = shifted
        else:
            flag = replica >> bit_number & 1 == 1
            feature_block = jnp.where(flag, shifted, feature_block)
    return feature_block


def move_up(feature_block):
    return passed_along(feature_block, "dom", -1)


def on_device(
    features, tile_weights, tile_rows, tile_cols, tile_counts, weight_self, weight_neigh, cotangent
):
    weights_dev = tile_weights[0, 0]
    rows_dev = tile_rows[0, 0]
    cols_dev = tile_cols[0, 0]
    counts_dev = tile_counts[0, 0]
    steps_per_group = weights_dev.shape[0]
    middle = steps_per_group // 2

    def contribution(feature_block, column_step):
        return step_terms(feature_block, weights_dev, rows_dev, cols_dev, counts_dev, column_step)

    empty = jnp.zeros(features.shape, jnp.float32)
    begin = rotate(features, steps_per_group, middle, -1)

    def turn_one(turn_index, carry):
        current, partial_value = carry
        partial_value = partial_value + contribution(current, turn_index)
        return (move_up(current), partial_value)

    current, partial_value = lax.fori_loop(0, steps_per_group - 1, turn_one, (begin, empty))
    partial_value = partial_value + contribution(current, steps_per_group - 1)
    aggregate = lax.psum_scatter(partial_value, "rep", scatter_dimension=0, tiled=True).astype(
        jnp.bfloat16
    )
    quarter = features.shape[0] // lax.axis_size("rep")
    own_rows = lax.dynamic_slice_in_dim(features, lax.axis_index("rep") * quarter, quarter, 0)
    pre = jnp.dot(own_rows, weight_self, preferred_element_type=jnp.float32)
    pre = pre + jnp.dot(aggregate, weight_neigh, preferred_element_type=jnp.float32)
    output = jax.nn.silu(pre).astype(jnp.bfloat16)
    sigmoid = jax.nn.sigmoid(pre)
    slope = (cotangent.astype(jnp.float32) * sigmoid * (1.0 + pre * (1.0 - sigmoid))).astype(
        jnp.bfloat16
    )
    self_term = jnp.einsum("nf,ng->fg", own_rows, slope, preferred_element_type=jnp.float32)
    neigh_term = jnp.einsum("nf,ng->fg", aggregate, slope, preferred_element_type=jnp.float32)
    grad_self, grad_neigh = lax.psum((self_term, neigh_term), ("dom", "rep"))
    return (output, grad_self, grad_neigh)


def solution(mesh):
    return jax.shard_map(
        on_device,
        mesh=mesh,
        in_specs=(
            P("dom", None),
            P("dom", "rep", None, None, None, None),
            P("dom", "rep", None, None),
            P("dom", "rep", None, None),
            P("dom", "rep", None),
            P(),
            P(),
            P(("dom", "rep"), None),
        ),
        out_specs=(P(("dom", "rep"), None), P(), P()),
        check_vma=False,
    )
```

profile of v0, /device:TPU:1, one launch (start us, length us, event | category | flops | bytes accessed | tf_op | source)
XLA Modules:
  0.0 608.2 jit_solution(17502834930815847477)
XLA Ops:
  9.7 20.5 %collective-permute-done.1 = bf16[1536,256]{1,0:T(8,128)(2,1)S(1)} collective-permute-done((bf16[1536,256]{1,0:T(8,128)(2,1)}, bf16[1536,256]{1,0:T(8,128)(2,1)S(1)}, u32[]{:S(2)}, u32[]{:S(2)}) %collective-permute-start.1) | collective-permute-done | bytes 786464 | tf_op jit(solution)/shard_map/ppermute | solution.py:10
  31.3 18.3 %collective-permute-done.2 = bf16[1536,256]{1,0:T(8,128)(2,1)S(1)} collective-permute-done((bf16[1536,256]{1,0:T(8,128)(2,1)S(1)}, bf16[1536,256]{1,0:T(8,128)(2,1)S(1)}, u32[]{:S(2)}, u32[]{:S(2)}) %collective-permute-start.2) | collective-permute-done | bytes 786464 | tf_op jit(solution)/shard_map/ppermute | solution.py:10
  53.1 13.7 %collective-permute-done.3 = bf16[1536,256]{1,0:T(8,128)(2,1)S(1)} collective-permute-done((bf16[1536,256]{1,0:T(8,128)(2,1)S(1)}, bf16[1536,256]{1,0:T(8,128)(2,1)S(1)}, u32[]{:S(2)}, u32[]{:S(2)}) %collective-permute-start.3) | collective-permute-done | bytes 786464 | tf_op jit(solution)/shard_map/ppermute | solution.py:10
  67.8 301.9 %while.16 = (s32[]{:T(128)}, bf16[1536,256]{1,0:T(8,128)(2,1)}, f32[1536,256]{1,0:T(8,128)}, s32[8,88]{1,0:T(8,128)}, s32[8]{0:T(128)}, /*index=5*/bf16[8,88,128...) while((s32[]{:T(128)}, bf16[1536,256]{1,0:T(8,128)(2,1)}, f32[1536,256]{1,0:T(8,128)}, ...), condition=%wide.region_1.2_spmd.clone, body=%wide.region_0.1_spmd.clone.sunk | while | flops 1226312832 | bytes 88607792 | solution.py:82
  69.0 3.9 collective-permute-start
  77.4 7.8 %fusion.53 = f32[88,128,256]{2,1,0:T(8,128)} fusion(bf16[88,128,256]{2,1,0:T(8,128)(2,1)S(1)} %bitcast.64, bf16[8,88,128,128]{3,2,1,0:T(8,128)(2,1)} %get-tuple-element.244, s32[]{:T(128)} %get-tuple-element.230), kind=kOutput, calls=%fused_computation.1.clone.1 | convolution fusion | flops 738197504 | bytes 20185600 | tf_op jit(solution)/shard_map/while/body/eval_jaxpr/kij,kjf->kif/dot_general | solution.py:27
  85.2 16.1 %copy.23 = f32[11,8,128,256]{3,1,2,0:T(8,128)} copy(f32[11,8,128,256]{3,2,1,0:T(8,128)} %bitcast.62) | data formatting | bytes 23068672 | tf_op jit(solution)/shard_map/while
  102.5 6.7 %fusion.54 = f32[12,32768]{1,0:T(8,128)S(1)} fusion(f32[88,32768]{1,0:T(8,128)} %bitcast.61, s32[88]{0:T(128)S(1)} %get-tuple-element.220, pred[88]{0:T(512)(128)(4,1)S(1)} %iota_compare_fusion.11), kind=kOutput, calls=%fused_computation.9.clone.1 | convolution fusion | flops 415238208 | bytes 13107640 | tf_op jit(solution)/shard_map/while/body/eval_jaxpr/dot_general | solution.py:30
  119.4 7.8 %fusion.53 = f32[88,128,256]{2,1,0:T(8,128)} fusion(bf16[88,128,256]{2,1,0:T(8,128)(2,1)S(1)} %bitcast.64, bf16[8,88,128,128]{3,2,1,0:T(8,128)(2,1)} %get-tuple-element.244, s32[]{:T(128)} %get-tuple-element.230), kind=kOutput, calls=%fused_computation.1.clone.1 | convolution fusion | flops 738197504 | bytes 20185600 | tf_op jit(solution)/shard_map/while/body/eval_jaxpr/kij,kjf->kif/dot_general | solution.py:27
  127.2 16.1 %copy.23 = f32[11,8,128,256]{3,1,2,0:T(8,128)} copy(f32[11,8,128,256]{3,2,1,0:T(8,128)} %bitcast.62) | data formatting | bytes 23068672 | tf_op jit(solution)/shard_map/while
  144.6 6.7 %fusion.54 = f32[12,32768]{1,0:T(8,128)S(1)} fusion(f32[88,32768]{1,0:T(8,128)} %bitcast.61, s32[88]{0:T(128)S(1)} %get-tuple-element.220, pred[88]{0:T(512)(128)(4,1)S(1)} %iota_compare_fusion.11), kind=kOutput, calls=%fused_computation.9.clone.1 | convolution fusion | flops 415238208 | bytes 13107640 | tf_op jit(solution)/shard_map/while/body/eval_jaxpr/dot_general | solution.py:30
  152.6 3.2 select_add_fusion.2
  161.7 7.8 %fusion.53 = f32[88,128,256]{2,1,0:T(8,128)} fusion(bf16[88,128,256]{2,1,0:T(8,128)(2,1)S(1)} %bitcast.64, bf16[8,88,128,128]{3,2,1,0:T(8,128)(2,1)} %get-tuple-element.244, s32[]{:T(128)} %get-tuple-element.230), kind=kOutput, calls=%fused_computation.1.clone.1 | convolution fusion | flops 738197504 | bytes 20185600 | tf_op jit(solution)/shard_map/while/body/eval_jaxpr/kij,kjf->kif/dot_general | solution.py:27
  169.4 16.1 %copy.23 = f32[11,8,128,256]{3,1,2,0:T(8,128)} copy(f32[11,8,128,256]{3,2,1,0:T(8,128)} %bitcast.62) | data formatting | bytes 23068672 | tf_op jit(solution)/shard_map/while
  186.8 6.7 %fusion.54 = f32[12,32768]{1,0:T(8,128)S(1)} fusion(f32[88,32768]{1,0:T(8,128)} %bitcast.61, s32[88]{0:T(128)S(1)} %get-tuple-element.220, pred[88]{0:T(512)(128)(4,1)S(1)} %iota_compare_fusion.11), kind=kOutput, calls=%fused_computation.9.clone.1 | convolution fusion | flops 415238208 | bytes 13107640 | tf_op jit(solution)/shard_map/while/body/eval_jaxpr/dot_general | solution.py:30
  203.9 7.8 %fusion.53 = f32[88,128,256]{2,1,0:T(8,128)} fusion(bf16[88,128,256]{2,1,0:T(8,128)(2,1)S(1)} %bitcast.64, bf16[8,88,128,128]{3,2,1,0:T(8,128)(2,1)} %get-tuple-element.244, s32[]{:T(128)} %get-tuple-element.230), kind=kOutput, calls=%fused_computation.1.clone.1 | convolution fusion | flops 738197504 | bytes 20185600 | tf_op jit(solution)/shard_map/while/body/eval_jaxpr/kij,kjf->kif/dot_general | solution.py:27
  211.7 16.1 %copy.23 = f32[11,8,128,256]{3,1,2,0:T(8,128)} copy(f32[11,8,128,256]{3,2,1,0:T(8,128)} %bitcast.62) | data formatting | bytes 23068672 | tf_op jit(solution)/shard_map/while
  229.0 6.7 %fusion.54 = f32[12,32768]{1,0:T(8,128)S(1)} fusion(f32[88,32768]{1,0:T(8,128)} %bitcast.61, s32[88]{0:T(128)S(1)} %get-tuple-element.220, pred[88]{0:T(512)(128)(4,1)S(1)} %iota_compare_fusion.11), kind=kOutput, calls=%fused_computation.9.clone.1 | convolution fusion | flops 415238208 | bytes 13107640 | tf_op jit(solution)/shard_map/while/body/eval_jaxpr/dot_general | solution.py:30
  248.5 7.8 %fusion.53 = f32[88,128,256]{2,1,0:T(8,128)} fusion(bf16[88,128,256]{2,1,0:T(8,128)(2,1)S(1)} %bitcast.64, bf16[8,88,128,128]{3,2,1,0:T(8,128)(2,1)} %get-tuple-element.244, s32[]{:T(128)} %get-tuple-element.230), kind=kOutput, calls=%fused_computation.1.clone.1 | convolution fusion | flops 738197504 | bytes 20185600 | tf_op jit(solution)/shard_map/while/body/eval_jaxpr/kij,kjf->kif/dot_general | solution.py:27
  256.3 16.1 %copy.23 = f32[11,8,128,256]{3,1,2,0:T(8,128)} copy(f32[11,8,128,256]{3,2,1,0:T(8,128)} %bitcast.62) | data formatting | bytes 23068672 | tf_op jit(solution)/shard_map/while
  273.7 6.7 %fusion.54 = f32[12,32768]{1,0:T(8,128)S(1)} fusion(f32[88,32768]{1,0:T(8,128)} %bitcast.61, s32[88]{0:T(128)S(1)} %get-tuple-element.220, pred[88]{0:T(512)(128)(4,1)S(1)} %iota_compare_fusion.11), kind=kOutput, calls=%fused_computation.9.clone.1 | convolution fusion | flops 415238208 | bytes 13107640 | tf_op jit(solution)/shard_map/while/body/eval_jaxpr/dot_general | solution.py:30
  291.0 7.8 %fusion.53 = f32[88,128,256]{2,1,0:T(8,128)} fusion(bf16[88,128,256]{2,1,0:T(8,128)(2,1)S(1)} %bitcast.64, bf16[8,88,128,128]{3,2,1,0:T(8,128)(2,1)} %get-tuple-element.244, s32[]{:T(128)} %get-tuple-element.230), kind=kOutput, calls=%fused_computation.1.clone.1 | convolution fusion | flops 738197504 | bytes 20185600 | tf_op jit(solution)/shard_map/while/body/eval_jaxpr/kij,kjf->kif/dot_general | solution.py:27
  298.8 16.1 %copy.23 = f32[11,8,128,256]{3,1,2,0:T(8,128)} copy(f32[11,8,128,256]{3,2,1,0:T(8,128)} %bitcast.62) | data formatting | bytes 23068672 | tf_op jit(solution)/shard_map/while
  316.2 6.7 %fusion.54 = f32[12,32768]{1,0:T(8,128)S(1)} fusion(f32[88,32768]{1,0:T(8,128)} %bitcast.61, s32[88]{0:T(128)S(1)} %get-tuple-element.220, pred[88]{0:T(512)(128)(4,1)S(1)} %iota_compare_fusion.11), kind=kOutput, calls=%fused_computation.9.clone.1 | convolution fusion | flops 415238208 | bytes 13107640 | tf_op jit(solution)/shard_map/while/body/eval_jaxpr/dot_general | solution.py:30
  333.3 7.8 %fusion.53 = f32[88,128,256]{2,1,0:T(8,128)} fusion(bf16[88,128,256]{2,1,0:T(8,128)(2,1)S(1)} %bitcast.64, bf16[8,88,128,128]{3,2,1,0:T(8,128)(2,1)} %get-tuple-element.244, s32[]{:T(128)} %get-tuple-element.230), kind=kOutput, calls=%fused_computation.1.clone.1 | convolution fusion | flops 738197504 | bytes 20185600 | tf_op jit(solution)/shard_map/while/body/eval_jaxpr/kij,kjf->kif/dot_general | solution.py:27
  341.1 16.1 %copy.23 = f32[11,8,128,256]{3,1,2,0:T(8,128)} copy(f32[11,8,128,256]{3,2,1,0:T(8,128)} %bitcast.62) | data formatting | bytes 23068672 | tf_op jit(solution)/shard_map/while
  358.4 6.7 %fusion.54 = f32[12,32768]{1,0:T(8,128)S(1)} fusion(f32[88,32768]{1,0:T(8,128)} %bitcast.61, s32[88]{0:T(128)S(1)} %get-tuple-element.220, pred[88]{0:T(512)(128)(4,1)S(1)} %iota_compare_fusion.11), kind=kOutput, calls=%fused_computation.9.clone.1 | convolution fusion | flops 415238208 | bytes 13107640 | tf_op jit(solution)/shard_map/while/body/eval_jaxpr/dot_general | solution.py:30
  374.5 8.6 %convolution_bitcast_fusion = f32[88,128,256]{1,2,0:T(8,128)} fusion(bf16[88,128,256]{2,1,0:T(8,128)(2,1)S(1)} %bitcast.68, bf16[1,1,8,88,128,128]{5,4,3,2,1,0:T(8,128)(2,1)} %bitcast.70), kind=kOutput, calls=%fused_computation.19 | convolution fusion | flops 738197504 | bytes 20185088 | tf_op jit(solution)/shard_map/kij,kjf->kif/dot_general | solution.py:27
  383.1 12.2 %copy.18 = f32[11,8,128,256]{3,1,2,0:T(8,128)} copy(f32[11,8,128,256]{2,3,1,0:T(8,128)} %bitcast.66) | data formatting | bytes 23068672
  395.3 8.2 %fusion.23 = f32[12,32768]{1,0:T(8,128)} fusion(f32[88,32768]{1,0:T(8,128)} %bitcast.65, s32[88]{0:T(128)S(1)} %slice_bitcast_fusion.1, pred[88]{0:T(512)(128)(4,1)S(1)} %iota_compare_fusion.7), kind=kOutput, calls=%fused_computation.39 | convolution fusion | flops 415238208 | bytes 13107640 | tf_op jit(solution)/shard_map/dot_general | solution.py:30
  407.9 37.6 %reduce-scatter.2.cloned.1.call-done = f32[384,256]{1,0:T(8,128)} async-done(((f32[1536,256]{1,0:T(8,128)}), f32[384,256]{1,0:T(8,128)}) %reduce-scatter.2.cloned.1.call-update) | async-done | bytes 393232 | tf_op jit(solution)/shard_map/reduce_scatter | solution.py:84
  451.5 146.5 %all-reduce.3.cloned.1.call-done = (f32[256,256]{1,0:T(8,128)}, f32[256,256]{1,0:T(8,128)}) async-done(((f32[256,256]{1,0:T(8,128)}, f32[256,256]{1,0:T(8,128)}), (f32[256,256]{1,0:T(8,128)}, f32[256,256]{1,0:T(8,128)})) %all-reduce.3.cloned.1.call-update) | async-done | bytes 524304 | tf_op jit(solution)/shard_map/psum | solution.py:98
  (120 shorter events, 106.8 us)
Async XLA Ops:
  7.2 438.4 %copy-start = (bf16[256,256]{1,0:T(8,128)(2,1)S(1)}, bf16[256,256]{1,0:T(8,128)(2,1)}, u32[]{:S(2)}) copy-start(bf16[256,256]{1,0:T(8,128)(2,1)} %param.16) | copy-start | bytes 393220
  7.2 438.4 %reduce-scatter.2.cloned.1.call-start = ((), (), s32[]{:S(2)}) async-start(), calls=%async_computation.1 | async-start | bytes 1966080 | tf_op jit(solution)/shard_map/reduce_scatter | solution.py:84
  7.2 23.0 %collective-permute-start.1 = (bf16[1536,256]{1,0:T(8,128)(2,1)}, bf16[1536,256]{1,0:T(8,128)(2,1)S(1)}, u32[]{:S(2)}, u32[]{:S(2)}) collective-permute-start(bf16[1536,256]{1,0:T(8,128)(2,1)} %param.10), channel_id=1, source_target_pairs={{112,0},{116,4},{120,8},{124,12},{0,16},{4,20},{8,24},{12,28},{16,... | collective-permute-start | bytes 2359304 | tf_op jit(solution)/shard_map/ppermute | solution.py:10
  30.3 19.4 %collective-permute-start.2 = (bf16[1536,256]{1,0:T(8,128)(2,1)S(1)}, bf16[1536,256]{1,0:T(8,128)(2,1)S(1)}, u32[]{:S(2)}, u32[]{:S(2)}) collective-permute-start(bf16[1536,256]{1,0:T(8,128)(2,1)S(1)} %collective-permute-done.1), channel_id=1, source_target_pairs={{32,0},{36,4},{40,8},{44,12},{48,16},{52,20},{56,24},{60,28},{64,3... | collective-permute-start | bytes 2359304 | tf_op jit(solution)/shard_map/ppermute | solution.py:10
  49.7 17.1 %collective-permute-start.3 = (bf16[1536,256]{1,0:T(8,128)(2,1)S(1)}, bf16[1536,256]{1,0:T(8,128)(2,1)S(1)}, u32[]{:S(2)}, u32[]{:S(2)}) collective-permute-start(bf16[1536,256]{1,0:T(8,128)(2,1)S(1)} %broadcast_select_fusion), channel_id=1, source_target_pairs={{64,0},{68,4},{72,8},{76,12},{80,16},{84,20},{88,24},{92,28},{96,3... | collective-permute-start | bytes 2359304 | tf_op jit(solution)/shard_map/ppermute | solution.py:10
  69.0 44.4 %collective-permute-start = (bf16[1536,256]{1,0:T(8,128)(2,1)S(1)}, bf16[1536,256]{1,0:T(8,128)(2,1)}, u32[]{:S(2)}, u32[]{:S(2)}) collective-permute-start(bf16[1536,256]{1,0:T(8,128)(2,1)S(1)} %copy.28), channel_id=1, source_target_pairs={{4,0},{8,4},{12,8},{16,12},{20,16},{24,20},{28,24},{32,28},{36,32}... | collective-permute-start | bytes 2359304 | tf_op jit(solution)/shard_map/while/body/eval_jaxpr/ppermute | solution.py:10
  85.2 16.1 %copy-start.3 = (s32[8]{0:T(128)S(1)}, s32[8]{0:T(128)}, u32[]{:S(2)}) copy-start(s32[8]{0:T(128)} %get-tuple-element.243) | copy-start | bytes 100 | tf_op jit(solution)/shard_map/while
  114.5 41.4 %collective-permute-start = (bf16[1536,256]{1,0:T(8,128)(2,1)S(1)}, bf16[1536,256]{1,0:T(8,128)(2,1)}, u32[]{:S(2)}, u32[]{:S(2)}) collective-permute-start(bf16[1536,256]{1,0:T(8,128)(2,1)S(1)} %copy.28), channel_id=1, source_target_pairs={{4,0},{8,4},{12,8},{16,12},{20,16},{24,20},{28,24},{32,28},{36,32}... | collective-permute-start | bytes 2359304 | tf_op jit(solution)/shard_map/while/body/eval_jaxpr/ppermute | solution.py:10
  127.2 16.1 %copy-start.3 = (s32[8]{0:T(128)S(1)}, s32[8]{0:T(128)}, u32[]{:S(2)}) copy-start(s32[8]{0:T(128)} %get-tuple-element.243) | copy-start | bytes 100 | tf_op jit(solution)/shard_map/while
  157.0 41.1 %collective-permute-start = (bf16[1536,256]{1,0:T(8,128)(2,1)S(1)}, bf16[1536,256]{1,0:T(8,128)(2,1)}, u32[]{:S(2)}, u32[]{:S(2)}) collective-permute-start(bf16[1536,256]{1,0:T(8,128)(2,1)S(1)} %copy.28), channel_id=1, source_target_pairs={{4,0},{8,4},{12,8},{16,12},{20,16},{24,20},{28,24},{32,28},{36,32}... | collective-permute-start | bytes 2359304 | tf_op jit(solution)/shard_map/while/body/eval_jaxpr/ppermute | solution.py:10
  169.4 16.1 %copy-start.3 = (s32[8]{0:T(128)S(1)}, s32[8]{0:T(128)}, u32[]{:S(2)}) copy-start(s32[8]{0:T(128)} %get-tuple-element.243) | copy-start | bytes 100 | tf_op jit(solution)/shard_map/while
  199.2 41.1 %collective-permute-start = (bf16[1536,256]{1,0:T(8,128)(2,1)S(1)}, bf16[1536,256]{1,0:T(8,128)(2,1)}, u32[]{:S(2)}, u32[]{:S(2)}) collective-permute-start(bf16[1536,256]{1,0:T(8,128)(2,1)S(1)} %copy.28), channel_id=1, source_target_pairs={{4,0},{8,4},{12,8},{16,12},{20,16},{24,20},{28,24},{32,28},{36,32}... | collective-permute-start | bytes 2359304 | tf_op jit(solution)/shard_map/while/body/eval_jaxpr/ppermute | solution.py:10
  211.7 16.1 %copy-start.3 = (s32[8]{0:T(128)S(1)}, s32[8]{0:T(128)}, u32[]{:S(2)}) copy-start(s32[8]{0:T(128)} %get-tuple-element.243) | copy-start | bytes 100 | tf_op jit(solution)/shard_map/while
  241.5 43.5 %collective-permute-start = (bf16[1536,256]{1,0:T(8,128)(2,1)S(1)}, bf16[1536,256]{1,0:T(8,128)(2,1)}, u32[]{:S(2)}, u32[]{:S(2)}) collective-permute-start(bf16[1536,256]{1,0:T(8,128)(2,1)S(1)} %copy.28), channel_id=1, source_target_pairs={{4,0},{8,4},{12,8},{16,12},{20,16},{24,20},{28,24},{32,28},{36,32}... | collective-permute-start | bytes 2359304 | tf_op jit(solution)/shard_map/while/body/eval_jaxpr/ppermute | solution.py:10
  256.3 16.1 %copy-start.3 = (s32[8]{0:T(128)S(1)}, s32[8]{0:T(128)}, u32[]{:S(2)}) copy-start(s32[8]{0:T(128)} %get-tuple-element.243) | copy-start | bytes 100 | tf_op jit(solution)/shard_map/while
  286.1 41.4 %collective-permute-start = (bf16[1536,256]{1,0:T(8,128)(2,1)S(1)}, bf16[1536,256]{1,0:T(8,128)(2,1)}, u32[]{:S(2)}, u32[]{:S(2)}) collective-permute-start(bf16[1536,256]{1,0:T(8,128)(2,1)S(1)} %copy.28), channel_id=1, source_target_pairs={{4,0},{8,4},{12,8},{16,12},{20,16},{24,20},{28,24},{32,28},{36,32}... | collective-permute-start | bytes 2359304 | tf_op jit(solution)/shard_map/while/body/eval_jaxpr/ppermute | solution.py:10
  298.8 16.1 %copy-start.3 = (s32[8]{0:T(128)S(1)}, s32[8]{0:T(128)}, u32[]{:S(2)}) copy-start(s32[8]{0:T(128)} %get-tuple-element.243) | copy-start | bytes 100 | tf_op jit(solution)/shard_map/while
  328.6 41.1 %collective-permute-start = (bf16[1536,256]{1,0:T(8,128)(2,1)S(1)}, bf16[1536,256]{1,0:T(8,128)(2,1)}, u32[]{:S(2)}, u32[]{:S(2)}) collective-permute-start(bf16[1536,256]{1,0:T(8,128)(2,1)S(1)} %copy.28), channel_id=1, source_target_pairs={{4,0},{8,4},{12,8},{16,12},{20,16},{24,20},{28,24},{32,28},{36,32}... | collective-permute-start | bytes 2359304 | tf_op jit(solution)/shard_map/while/body/eval_jaxpr/ppermute | solution.py:10
  341.1 16.1 %copy-start.3 = (s32[8]{0:T(128)S(1)}, s32[8]{0:T(128)}, u32[]{:S(2)}) copy-start(s32[8]{0:T(128)} %get-tuple-element.243) | copy-start | bytes 100 | tf_op jit(solution)/shard_map/while
  395.3 10.0 %copy-start.1 = (f32[1536,256]{1,0:T(8,128)S(1)}, f32[1536,256]{1,0:T(8,128)}, u32[]{:S(2)}) copy-start(f32[1536,256]{1,0:T(8,128)} %get-tuple-element.128) | copy-start | bytes 4718596
  403.5 3.3 copy-start.2
  406.7 191.2 %all-reduce.3.cloned.1.call-start = ((), (), s32[]{:S(2)}) async-start(), calls=%async_computation.2 | async-start | bytes 1048576 | tf_op jit(solution)/shard_map/psum | solution.py:98
Sparse Core Ops, SparseCore 0:
  406.9 38.6 reduce-scatter.1
  451.7 146.2 all-reduce.2
where the time goes:
time: 610 us; the launch traced here: 608 us
  waiting for transfers between devices  237 us (39%)
  local copies, waits for them, and re-layouts  177 us (29%)
  matrix products  139 us (23%)
  other arithmetic  29.8 us (5%)
  between operations  14.1 us (2%)
  starting transfers between devices  11.7 us (2%)
    psum x1, waiting for transfers between devices, on_device(): grad_self, grad_neigh = lax.psum((self_term, neigh_term), ('dom', 'rep'))  146 us
    while x35, local copies, waits for them, and re-layouts  132 us
    dot_general x8, matrix products, step_terms(): jnp.einsum('kij,kjf->kif', weights_now, picked, preferred_element_type=jn...  63.2 us
    dot_general x8, matrix products, step_terms(): jnp.dot(placing, product.reshape(slot_total, tile_side * width), precisio...  55 us
    ppermute x10, waiting for transfers between devices, passed_along(): return lax.ppermute(block, axis, route)  52.5 us
    reduce_scatter x1, waiting for transfers between devices, on_device(): lax.psum_scatter(partial_value, 'rep', scatter_dimension=0, tiled=True)  37.6 us
    add x7, other arithmetic, turn_one(): partial_value = partial_value + contribution(current, turn_index)  22.1 us
    unnamed x10, local copies, waits for them, and re-layouts  17.1 us
  transfers between devices with their start and end apart: 12, of which 5 were waited for; matrix products, arithmetic and copies ran while one was open for 48% of the time, Pallas kernels for 0%

commit v1 on v0

--- a/solution.py
+++ b/solution.py
@@ -95,7 +95,7 @@
     )
     self_term = jnp.einsum("nf,ng->fg", own_rows, slope, preferred_element_type=jnp.float32)
     neigh_term = jnp.einsum("nf,ng->fg", aggregate, slope, preferred_element_type=jnp.float32)
-    grad_self, grad_neigh = lax.psum((self_term, neigh_term), ("dom", "rep"))
+    grad_self, grad_neigh = lax.psum(lax.psum((self_term, neigh_term), "dom"), "rep")
     return (output, grad_self, grad_neigh)
 
 

time: 610 us -> 819 us (1.34)
  waiting for transfers between devices: 237 us -> 446 us
    psum x1 -> x2, waiting for transfers between devices: 146 us -> 355 us  [the longest x1 289 us: on_device(): lax.psum((self_term, neigh_term), 'dom')]
  transfers between devices with their start and end apart: 12 -> 13, of which waited for: 5 -> 6; matrix products, arithmetic and copies ran while one was open for 48% -> 36% of each run, Pallas kernels for 0% -> 0%
where the time goes in v1:
time: 819 us; the launch traced here: 817 us
  waiting for transfers between devices  446 us (54%)
  local copies, waits for them, and re-layouts  177 us (22%)
  matrix products  139 us (17%)
  other arithmetic  29.9 us (4%)
  between operations  13.8 us (2%)
  starting transfers between devices  11.7 us (1%)
    psum x1, waiting for transfers between devices, on_device(): lax.psum((self_term, neigh_term), 'dom')  289 us
    while x35, local copies, waits for them, and re-layouts  132 us
    psum x1, waiting for transfers between devices, on_device(): lax.psum(lax.psum((self_term, neigh_term), 'dom'), 'rep')  66.8 us
    dot_general x8, matrix products, step_terms(): jnp.einsum('kij,kjf->kif', weights_now, picked, preferred_element_type=jn...  63.2 us
    dot_general x8, matrix products, step_terms(): jnp.dot(placing, product.reshape(slot_total, tile_side * width), precisio...  55 us
    ppermute x10, waiting for transfers between devices, passed_along(): return lax.ppermute(block, axis, route)  52.5 us
    reduce_scatter x1, waiting for transfers between devices, on_device(): lax.psum_scatter(partial_value, 'rep', scatter_dimension=0, tiled=True)  37.6 us
    add x7, other arithmetic, turn_one(): partial_value = partial_value + contribution(current, turn_index)  22.2 us
  transfers between devices with their start and end apart: 13, of which 6 were waited for; matrix products, arithmetic and copies ran while one was open for 36% of the time, Pallas kernels for 0%

profile of v1, /device:TPU:1, one launch (start us, length us, event | category | flops | bytes accessed | tf_op | source)
XLA Modules:
  0.0 817.0 jit_solution(10863706267927850097)
XLA Ops:
  9.7 20.5 %collective-permute-done.1 = bf16[1536,256]{1,0:T(8,128)(2,1)S(1)} collective-permute-done((bf16[1536,256]{1,0:T(8,128)(2,1)}, bf16[1536,256]{1,0:T(8,128)(2,1)S(1)}, u32[]{:S(2)}, u32[]{:S(2)}) %collective-permute-start.1) | collective-permute-done | bytes 786464 | tf_op jit(solution)/shard_map/ppermute | solution.py:10
  31.3 18.3 %collective-permute-done.2 = bf16[1536,256]{1,0:T(8,128)(2,1)S(1)} collective-permute-done((bf16[1536,256]{1,0:T(8,128)(2,1)S(1)}, bf16[1536,256]{1,0:T(8,128)(2,1)S(1)}, u32[]{:S(2)}, u32[]{:S(2)}) %collective-permute-start.2) | collective-permute-done | bytes 786464 | tf_op jit(solution)/shard_map/ppermute | solution.py:10
  53.1 13.7 %collective-permute-done.3 = bf16[1536,256]{1,0:T(8,128)(2,1)S(1)} collective-permute-done((bf16[1536,256]{1,0:T(8,128)(2,1)S(1)}, bf16[1536,256]{1,0:T(8,128)(2,1)S(1)}, u32[]{:S(2)}, u32[]{:S(2)}) %collective-permute-start.3) | collective-permute-done | bytes 786464 | tf_op jit(solution)/shard_map/ppermute | solution.py:10
  67.8 302.1 %while.16 = (s32[]{:T(128)}, bf16[1536,256]{1,0:T(8,128)(2,1)}, f32[1536,256]{1,0:T(8,128)}, s32[8,88]{1,0:T(8,128)}, s32[8]{0:T(128)}, /*index=5*/bf16[8,88,128...) while((s32[]{:T(128)}, bf16[1536,256]{1,0:T(8,128)(2,1)}, f32[1536,256]{1,0:T(8,128)}, ...), condition=%wide.region_1.2_spmd.clone, body=%wide.region_0.1_spmd.clone.sunk | while | flops 1226312832 | bytes 88607792 | solution.py:82
  68.9 3.9 collective-permute-start
  77.4 7.8 fusion.53
  85.2 16.1 %copy.23 = f32[11,8,128,256]{3,1,2,0:T(8,128)} copy(f32[11,8,128,256]{3,2,1,0:T(8,128)} %bitcast.62) | data formatting | bytes 23068672 | tf_op jit(solution)/shard_map/while
  102.5 6.7 fusion.54
  119.4 7.8 fusion.53
  127.2 16.1 %copy.23 = f32[11,8,128,256]{3,1,2,0:T(8,128)} copy(f32[11,8,128,256]{3,2,1,0:T(8,128)} %bitcast.62) | data formatting | bytes 23068672 | tf_op jit(solution)/shard_map/while
  144.6 6.7 fusion.54
  161.7 7.8 fusion.53
  169.5 16.1 %copy.23 = f32[11,8,128,256]{3,1,2,0:T(8,128)} copy(f32[11,8,128,256]{3,2,1,0:T(8,128)} %bitcast.62) | data formatting | bytes 23068672 | tf_op jit(solution)/shard_map/while
  186.9 6.7 fusion.54
  203.9 7.8 fusion.53
  211.7 16.1 %copy.23 = f32[11,8,128,256]{3,1,2,0:T(8,128)} copy(f32[11,8,128,256]{3,2,1,0:T(8,128)} %bitcast.62) | data formatting | bytes 23068672 | tf_op jit(solution)/shard_map/while
  229.1 6.7 fusion.54
  248.6 7.8 fusion.53
  256.4 16.1 %copy.23 = f32[11,8,128,256]{3,1,2,0:T(8,128)} copy(f32[11,8,128,256]{3,2,1,0:T(8,128)} %bitcast.62) | data formatting | bytes 23068672 | tf_op jit(solution)/shard_map/while
  273.8 6.7 fusion.54
  291.1 7.8 fusion.53
  299.0 16.1 %copy.23 = f32[11,8,128,256]{3,1,2,0:T(8,128)} copy(f32[11,8,128,256]{3,2,1,0:T(8,128)} %bitcast.62) | data formatting | bytes 23068672 | tf_op jit(solution)/shard_map/while
  316.3 6.7 fusion.54
  333.4 7.8 fusion.53
  341.2 16.1 %copy.23 = f32[11,8,128,256]{3,1,2,0:T(8,128)} copy(f32[11,8,128,256]{3,2,1,0:T(8,128)} %bitcast.62) | data formatting | bytes 23068672 | tf_op jit(solution)/shard_map/while
  358.6 6.7 fusion.54
  374.7 8.6 %convolution_bitcast_fusion = f32[88,128,256]{1,2,0:T(8,128)} fusion(bf16[88,128,256]{2,1,0:T(8,128)(2,1)S(1)} %bitcast.68, bf16[1,1,8,88,128,128]{5,4,3,2,1,0:T(8,128)(2,1)} %bitcast.70), kind=kOutput, calls=%fused_computation.19 | convolution fusion | flops 738197504 | bytes 20185088 | tf_op jit(solution)/shard_map/kij,kjf->kif/dot_general | solution.py:27
  383.3 12.2 %copy.18 = f32[11,8,128,256]{3,1,2,0:T(8,128)} copy(f32[11,8,128,256]{2,3,1,0:T(8,128)} %bitcast.66) | data formatting | bytes 23068672
  395.5 8.1 fusion.23
  408.1 37.6 %reduce-scatter.2.cloned.1.call-done = f32[384,256]{1,0:T(8,128)} async-done(((f32[1536,256]{1,0:T(8,128)}), f32[384,256]{1,0:T(8,128)}) %reduce-scatter.2.cloned.1.call-update) | async-done | bytes 393232 | tf_op jit(solution)/shard_map/reduce_scatter | solution.py:84
  451.7 288.6 %all-reduce.5.cloned.1.call-done = (f32[256,256]{1,0:T(8,128)}, f32[256,256]{1,0:T(8,128)}) async-done(((f32[256,256]{1,0:T(8,128)}, f32[256,256]{1,0:T(8,128)}), (f32[256,256]{1,0:T(8,128)}, f32[256,256]{1,0:T(8,128)})) %all-reduce.5.cloned.1.call-update) | async-done | bytes 524304 | tf_op jit(solution)/shard_map/psum | solution.py:98
  740.3 66.8 %all-reduce.7.cloned.1.call-done = (f32[256,256]{1,0:T(8,128)}, f32[256,256]{1,0:T(8,128)}) async-done(((f32[256,256]{1,0:T(8,128)}, f32[256,256]{1,0:T(8,128)}), (f32[256,256]{1,0:T(8,128)}, f32[256,256]{1,0:T(8,128)})) %all-reduce.7.cloned.1.call-update) | async-done | bytes 524304 | tf_op jit(solution)/shard_map/psum | solution.py:98
  (123 shorter events, 110.1 us)
Async XLA Ops:
  7.2 438.5 %copy-start = (bf16[256,256]{1,0:T(8,128)(2,1)S(1)}, bf16[256,256]{1,0:T(8,128)(2,1)}, u32[]{:S(2)}) copy-start(bf16[256,256]{1,0:T(8,128)(2,1)} %param.16) | copy-start | bytes 393220
  7.2 438.5 %reduce-scatter.2.cloned.1.call-start = ((), (), s32[]{:S(2)}) async-start(), calls=%async_computation.1 | async-start | bytes 1966080 | tf_op jit(solution)/shard_map/reduce_scatter | solution.py:84
  7.2 23.0 %collective-permute-start.1 = (bf16[1536,256]{1,0:T(8,128)(2,1)}, bf16[1536,256]{1,0:T(8,128)(2,1)S(1)}, u32[]{:S(2)}, u32[]{:S(2)}) collective-permute-start(bf16[1536,256]{1,0:T(8,128)(2,1)} %param.10), channel_id=1, source_target_pairs={{112,0},{116,4},{120,8},{124,12},{0,16},{4,20},{8,24},{12,28},{16,... | collective-permute-start | bytes 2359304 | tf_op jit(solution)/shard_map/ppermute | solution.py:10
  30.3 19.4 %collective-permute-start.2 = (bf16[1536,256]{1,0:T(8,128)(2,1)S(1)}, bf16[1536,256]{1,0:T(8,128)(2,1)S(1)}, u32[]{:S(2)}, u32[]{:S(2)}) collective-permute-start(bf16[1536,256]{1,0:T(8,128)(2,1)S(1)} %collective-permute-done.1), channel_id=1, source_target_pairs={{32,0},{36,4},{40,8},{44,12},{48,16},{52,20},{56,24},{60,28},{64,3... | collective-permute-start | bytes 2359304 | tf_op jit(solution)/shard_map/ppermute | solution.py:10
  49.7 17.1 %collective-permute-start.3 = (bf16[1536,256]{1,0:T(8,128)(2,1)S(1)}, bf16[1536,256]{1,0:T(8,128)(2,1)S(1)}, u32[]{:S(2)}, u32[]{:S(2)}) collective-permute-start(bf16[1536,256]{1,0:T(8,128)(2,1)S(1)} %broadcast_select_fusion), channel_id=1, source_target_pairs={{64,0},{68,4},{72,8},{76,12},{80,16},{84,20},{88,24},{92,28},{96,3... | collective-permute-start | bytes 2359304 | tf_op jit(solution)/shard_map/ppermute | solution.py:10
  68.9 44.4 %collective-permute-start = (bf16[1536,256]{1,0:T(8,128)(2,1)S(1)}, bf16[1536,256]{1,0:T(8,128)(2,1)}, u32[]{:S(2)}, u32[]{:S(2)}) collective-permute-start(bf16[1536,256]{1,0:T(8,128)(2,1)S(1)} %copy.28), channel_id=1, source_target_pairs={{4,0},{8,4},{12,8},{16,12},{20,16},{24,20},{28,24},{32,28},{36,32}... | collective-permute-start | bytes 2359304 | tf_op jit(solution)/shard_map/while/body/eval_jaxpr/ppermute | solution.py:10
  85.2 16.1 %copy-start.3 = (s32[8]{0:T(128)S(1)}, s32[8]{0:T(128)}, u32[]{:S(2)}) copy-start(s32[8]{0:T(128)} %get-tuple-element.245) | copy-start | bytes 100 | tf_op jit(solution)/shard_map/while
  114.5 41.4 %collective-permute-start = (bf16[1536,256]{1,0:T(8,128)(2,1)S(1)}, bf16[1536,256]{1,0:T(8,128)(2,1)}, u32[]{:S(2)}, u32[]{:S(2)}) collective-permute-start(bf16[1536,256]{1,0:T(8,128)(2,1)S(1)} %copy.28), channel_id=1, source_target_pairs={{4,0},{8,4},{12,8},{16,12},{20,16},{24,20},{28,24},{32,28},{36,32}... | collective-permute-start | bytes 2359304 | tf_op jit(solution)/shard_map/while/body/eval_jaxpr/ppermute | solution.py:10
  127.2 16.1 %copy-start.3 = (s32[8]{0:T(128)S(1)}, s32[8]{0:T(128)}, u32[]{:S(2)}) copy-start(s32[8]{0:T(128)} %get-tuple-element.245) | copy-start | bytes 100 | tf_op jit(solution)/shard_map/while
  157.0 41.1 %collective-permute-start = (bf16[1536,256]{1,0:T(8,128)(2,1)S(1)}, bf16[1536,256]{1,0:T(8,128)(2,1)}, u32[]{:S(2)}, u32[]{:S(2)}) collective-permute-start(bf16[1536,256]{1,0:T(8,128)(2,1)S(1)} %copy.28), channel_id=1, source_target_pairs={{4,0},{8,4},{12,8},{16,12},{20,16},{24,20},{28,24},{32,28},{36,32}... | collective-permute-start | bytes 2359304 | tf_op jit(solution)/shard_map/while/body/eval_jaxpr/ppermute | solution.py:10
  169.5 16.1 %copy-start.3 = (s32[8]{0:T(128)S(1)}, s32[8]{0:T(128)}, u32[]{:S(2)}) copy-start(s32[8]{0:T(128)} %get-tuple-element.245) | copy-start | bytes 100 | tf_op jit(solution)/shard_map/while
  199.3 41.1 %collective-permute-start = (bf16[1536,256]{1,0:T(8,128)(2,1)S(1)}, bf16[1536,256]{1,0:T(8,128)(2,1)}, u32[]{:S(2)}, u32[]{:S(2)}) collective-permute-start(bf16[1536,256]{1,0:T(8,128)(2,1)S(1)} %copy.28), channel_id=1, source_target_pairs={{4,0},{8,4},{12,8},{16,12},{20,16},{24,20},{28,24},{32,28},{36,32}... | collective-permute-start | bytes 2359304 | tf_op jit(solution)/shard_map/while/body/eval_jaxpr/ppermute | solution.py:10
  211.7 16.1 %copy-start.3 = (s32[8]{0:T(128)S(1)}, s32[8]{0:T(128)}, u32[]{:S(2)}) copy-start(s32[8]{0:T(128)} %get-tuple-element.245) | copy-start | bytes 100 | tf_op jit(solution)/shard_map/while
  241.5 43.5 %collective-permute-start = (bf16[1536,256]{1,0:T(8,128)(2,1)S(1)}, bf16[1536,256]{1,0:T(8,128)(2,1)}, u32[]{:S(2)}, u32[]{:S(2)}) collective-permute-start(bf16[1536,256]{1,0:T(8,128)(2,1)S(1)} %copy.28), channel_id=1, source_target_pairs={{4,0},{8,4},{12,8},{16,12},{20,16},{24,20},{28,24},{32,28},{36,32}... | collective-permute-start | bytes 2359304 | tf_op jit(solution)/shard_map/while/body/eval_jaxpr/ppermute | solution.py:10
  256.4 16.1 %copy-start.3 = (s32[8]{0:T(128)S(1)}, s32[8]{0:T(128)}, u32[]{:S(2)}) copy-start(s32[8]{0:T(128)} %get-tuple-element.245) | copy-start | bytes 100 | tf_op jit(solution)/shard_map/while
  286.2 41.4 %collective-permute-start = (bf16[1536,256]{1,0:T(8,128)(2,1)S(1)}, bf16[1536,256]{1,0:T(8,128)(2,1)}, u32[]{:S(2)}, u32[]{:S(2)}) collective-permute-start(bf16[1536,256]{1,0:T(8,128)(2,1)S(1)} %copy.28), channel_id=1, source_target_pairs={{4,0},{8,4},{12,8},{16,12},{20,16},{24,20},{28,24},{32,28},{36,32}... | collective-permute-start | bytes 2359304 | tf_op jit(solution)/shard_map/while/body/eval_jaxpr/ppermute | solution.py:10
  298.9 16.1 %copy-start.3 = (s32[8]{0:T(128)S(1)}, s32[8]{0:T(128)}, u32[]{:S(2)}) copy-start(s32[8]{0:T(128)} %get-tuple-element.245) | copy-start | bytes 100 | tf_op jit(solution)/shard_map/while
  328.8 41.1 %collective-permute-start = (bf16[1536,256]{1,0:T(8,128)(2,1)S(1)}, bf16[1536,256]{1,0:T(8,128)(2,1)}, u32[]{:S(2)}, u32[]{:S(2)}) collective-permute-start(bf16[1536,256]{1,0:T(8,128)(2,1)S(1)} %copy.28), channel_id=1, source_target_pairs={{4,0},{8,4},{12,8},{16,12},{20,16},{24,20},{28,24},{32,28},{36,32}... | collective-permute-start | bytes 2359304 | tf_op jit(solution)/shard_map/while/body/eval_jaxpr/ppermute | solution.py:10
  341.2 16.1 %copy-start.3 = (s32[8]{0:T(128)S(1)}, s32[8]{0:T(128)}, u32[]{:S(2)}) copy-start(s32[8]{0:T(128)} %get-tuple-element.245) | copy-start | bytes 100 | tf_op jit(solution)/shard_map/while
  395.5 10.0 %copy-start.1 = (f32[1536,256]{1,0:T(8,128)S(1)}, f32[1536,256]{1,0:T(8,128)}, u32[]{:S(2)}) copy-start(f32[1536,256]{1,0:T(8,128)} %get-tuple-element.128) | copy-start | bytes 4718596
  403.6 3.3 copy-start.2
  406.9 333.4 %all-reduce.5.cloned.1.call-start = ((), (), s32[]{:S(2)}) async-start(), calls=%async_computation.2 | async-start | bytes 1048576 | tf_op jit(solution)/shard_map/psum | solution.py:98
  451.6 355.5 %all-reduce.7.cloned.1.call-start = ((), (), s32[]{:S(2)}) async-start(), calls=%async_computation.3 | async-start | bytes 1048576 | tf_op jit(solution)/shard_map/psum | solution.py:98
Sparse Core Ops, SparseCore 0:
  407.0 38.5 reduce-scatter.1
  451.8 288.5 all-reduce.4
  742.9 64.1 all-reduce.6
